TPU v7x, 32 devices: a whole 2x2x4 slice. The times are simulated.
32 devices in a mesh: tok: 8 (over z, x), col: 4 (over y, core).
Axes of the slice: x: 2, y: 2, z: 4, core: 2. Of those that a mesh axis runs over, the one named last changes fastest.
Arguments:
- tokens: bfloat16 [2560, 4096], P('tok', 'col'), may hold values from -16 to 16
- w_query: bfloat16 [4096, 2048], P(None, 'col'), may hold values from -0.09375 to 0.09375
- w_key: bfloat16 [4096, 512], P(None, 'col'), may hold values from -0.09375 to 0.09375
- w_value: bfloat16 [4096, 512], P(None, 'col'), may hold values from -0.09375 to 0.09375
- w_out: bfloat16 [2048, 4096], P('col'), may hold values from -0.125 to 0.125
- block_ids: int32 [16, 40, 16], P('col', 'tok'), may hold values from 0 to 39, as said below
- block_counts: int32 [16, 40], P('col', 'tok'), may hold values from 1 to 16, as said below
Outputs:
- mixed: bfloat16 [2560, 4096], P('tok', 'col')
Inputs may be any that keep to these rules, and one draw needn't show every extreme that they name: block_ids[h, b, 0] = b; the slots below block_counts[h, b] hold distinct blocks none after b; later slots hold block numbers that are not read. block_counts[h, b] <= b + 1; densities differ from head to head, and some row of some head uses all 16 slots.
All inputs are finite; a program needn't handle non-finite values.
Results may differ from a plain program's by a relative error of at most 0.012.
Values may be sent and summed in bfloat16 or wider, within the bound.
No kernel may reach another device: no remote copies, remote signals or barrier semaphores. Data moves between devices by JAX's collectives and lax.ppermute only.
A program may use at most 64 MiB of HBM per device.

v0:
```python
import jax
import jax.numpy as jnp
from jax import lax
from jax.sharding import PartitionSpec as P

HEAD_SIZE = 128
BLK = 64
NSEL = 16
rope_base = 500000.0


def rotate(field, positions):
    half = field.shape[-1] // 2
    freq = rope_base ** (-jnp.arange(half, dtype=jnp.float32) / half)
    angle = positions[:, None] * freq[None, :]
    cosine = jnp.cos(angle)[:, None, :]
    sine = jnp.sin(angle)[:, None, :]
    first = field[..., :half]
    second = field[..., half:]
    return jnp.concatenate(
        [first * cosine - second * sine, second * cosine + first * sine], axis=-1
    )


def on_device(tokens, w_query, w_key, w_value, w_out, block_ids, block_counts):
    tok_rows = tokens.shape[0]
    head_local = w_query.shape[1] // HEAD_SIZE
    kv_local = w_key.shape[1] // HEAD_SIZE
    group_size = head_local // kv_local
    blocks_dev = block_ids.shape[1]
    piece = lax.all_gather(tokens, "col", axis=1, tiled=True)
    width = piece.shape[1]

    def product(weight):
        return jnp.dot(piece, weight, preferred_element_type=jnp.float32)

    query_raw = product(w_query)
    key_raw = product(w_key)
    value_raw = product(w_value)
    tok_place = lax.axis_index("tok")
    query_index = tok_place * tok_rows + jnp.arange(tok_rows, dtype=jnp.int32)
    positions = query_index.astype(jnp.float32)
    query_rows = rotate(query_raw.reshape(tok_rows, head_local, HEAD_SIZE), positions).astype(
        jnp.bfloat16
    )
    keys = rotate(key_raw.reshape(tok_rows, kv_local, HEAD_SIZE), positions).astype(jnp.bfloat16)
    values = value_raw.astype(jnp.bfloat16).reshape(tok_rows, kv_local, HEAD_SIZE)
    grouped = query_rows.reshape(tok_rows, kv_local, group_size, HEAD_SIZE)
    live = jnp.arange(NSEL, dtype=jnp.int32)[None, None, :] < block_counts[:, :, None]
    last_query = tok_place * tok_rows + tok_rows - 1
    start_state = (
        jnp.full((head_local, tok_rows), -1e30, jnp.float32),
        jnp.zeros((head_local, tok_rows), jnp.float32),
        jnp.zeros((head_local, tok_rows, HEAD_SIZE), jnp.float32),
    )
    key_part = lax.all_gather(keys, "tok", axis=0, tiled=True)
    value_part = lax.all_gather(values, "tok", axis=0, tiled=True)
    amount = key_part.shape[0]
    width = 512
    key_blocks = key_part.reshape(amount // width, width, kv_local, HEAD_SIZE)
    value_blocks = value_part.reshape(amount // width, width, kv_local, HEAD_SIZE)
    offsets = jnp.arange(amount // width, dtype=jnp.int32) * width

    def one_block(state, inputs):
        key_block, value_block, offset = inputs

        def compute(inner_state):
            highest, total, summed_weights = inner_state
            key_index = offset + jnp.arange(width, dtype=jnp.int32)
            key_group = key_index // BLK
            hit = jnp.any(
                (block_ids[:, :, :, None] == key_group[None, None, None, :]) & live[..., None],
                axis=2,
            )
            allowed = jnp.broadcast_to(hit[:, :, None, :], (head_local, blocks_dev, BLK, width))
            allowed = allowed.reshape(head_local, tok_rows, width)
            allowed = allowed & (key_index[None, None, :] <= query_index[None, :, None])
            logit_scores = jnp.einsum(
                "tcgd,kcd->cgtk", grouped, key_block, preferred_element_type=jnp.float32
            )
            logit_scores = logit_scores.reshape(head_local, tok_rows, width) * HEAD_SIZE ** (-0.5)
            masked = jnp.where(allowed, logit_scores, -1e30)
            fresh = jnp.maximum(highest, jnp.max(masked, axis=-1))
            decay = jnp.exp(highest - fresh)
            weights = jnp.where(allowed, jnp.exp(masked - fresh[..., None]), 0.0)
            total = total * decay + jnp.sum(weights, axis=-1)
            rounded_scores = weights.astype(jnp.bfloat16).reshape(
                kv_local, group_size, tok_rows, width
            )
            added = jnp.einsum(
                "cgtk,kcd->cgtd", rounded_scores, value_block, preferred_element_type=jnp.float32
            )
            summed_weights = summed_weights * decay[..., None] + added.reshape(
                head_local, tok_rows, HEAD_SIZE
            )
            return (fresh, total, summed_weights)

        return (
            lax.cond(offset > last_query, lambda inner_state: inner_state, compute, state),
            None,
        )

    result, _ = lax.scan(one_block, start_state, (key_blocks, value_blocks, offsets))
    highest, total, summed_weights = result
    attended = jnp.transpose((summed_weights / total[..., None]).astype(jnp.bfloat16), (1, 0, 2))
    flat = attended.reshape(tok_rows, head_local * HEAD_SIZE)
    summed_out = lax.psum_scatter(
        lax.dot_general(
            w_out, flat, (((0,), (1,)), ((), ())), preferred_element_type=jnp.float32
        ).astype(jnp.bfloat16),
        "col",
        scatter_dimension=0,
        tiled=True,
    ).astype(jnp.float32)
    return jnp.transpose(summed_out).astype(jnp.bfloat16)


def solution(mesh):
    in_specs = (
        P("tok", "col"),
        P(None, "col"),
        P(None, "col"),
        P(None, "col"),
        P("col", None),
        P("col", "tok", None),
        P("col", "tok"),
    )
    out_specs = P("tok", "col")
    return jax.shard_map(
        on_device, mesh=mesh, in_specs=in_specs, out_specs=out_specs, check_vma=False
    )
```

profile of v0, /device:TPU:0, one launch (start us, length us, event | category | flops | bytes accessed | tf_op | source)
XLA Modules:
  0.0 185.4 jit_solution(4791514653528160586)
XLA Ops:
  6.5 0.0 copy-start
  6.5 0.0 all-gather.3.cloned.1.call-start
  6.5 0.7 all-gather.3.cloned.1.call-update
  7.3 0.0 reduce-scatter.2.cloned.1.call-start
  7.3 0.7 copy.25
  8.0 0.6 multiply_cosine_fusion
  8.7 28.5 %all-gather.3.cloned.1.call-done = bf16[320,4096]{1,0:T(8,128)(2,1)} async-done(((bf16[320,1024]{1,0:T(8,128)(2,1)}), bf16[320,4096]{1,0:T(8,128)(2,1)}) %all-gather.3.cloned.1.call-update) | async-done | bytes 2621456 | tf_op jit(solution)/shard_map/all_gather | solution.py:31
  37.2 4.5 %fusion.43 = f32[320,512]{1,0:T(8,128)S(1)} fusion(bf16[320,4096]{1,0:T(8,128)(2,1)} %all-gather.3.cloned.1.call-done, bf16[4096,512]{1,0:T(8,128)(2,1)} %param.12), kind=kOutput, calls=%fused_computation.67 | convolution fusion | flops 1342177280 | bytes 7471104 | tf_op jit(solution)/shard_map/dot_general | solution.py:35
  41.7 0.2 reshape.338
  41.9 0.0 copy-start.1
  41.9 0.4 fusion.42
  42.3 0.0 copy-done
  42.3 1.3 copy-done.1
  43.7 0.0 copy-start.2
  43.7 0.8 convolution_bitcast_fusion
  44.5 0.7 fusion.39
  45.2 0.1 pad_maximum_fusion.1
  45.3 31.9 %all_gather.10 = bf16[2560,1,128]{2,0,1:T(8,128)(2,1)S(1)} all-gather(bf16[320,1,128]{2,0,1:T(8,128)(2,1)S(1)} %pad_maximum_fusion.1), channel_id=1, replica_groups=mesh['tok'=8,'col'=4] {'tok'}, dimensions={0}, use_global_device_ids=true | all-gather | bytes 737280 | tf_op jit(solution)/shard_map/all_gather | solution.py:56
  77.3 0.0 copy-done.2
  77.3 0.8 convolution_convert_fusion.1
  78.1 0.0 copy-start.3
  78.2 31.4 %all-gather = bf16[2560,128]{1,0:T(8,128)(2,1)S(1)} all-gather(bf16[320,128]{1,0:T(8,128)(2,1)S(1)} %convolution_convert_fusion.1), channel_id=2, replica_groups=mesh['tok'=8,'col'=4] {'tok'}, dimensions={0}, use_global_device_ids=true | all-gather | bytes 737280 | tf_op jit(solution)/shard_map/all_gather | solution.py:57
  109.6 0.2 fusion.29
  109.7 0.2 pad_maximum_fusion
  110.0 0.0 copy-done.3
  110.0 11.1 %while.15 = (s32[]{:T(128)}, f32[4,320]{1,0:T(4,128)S(1)}, f32[4,320]{1,0:T(4,128)S(1)}, f32[4,320,128]{2,1,0:T(8,128)S(1)}, s32[5]{0:T(128)S(1)}, /*index=5*/s3...) while((s32[]{:T(128)}, f32[4,320]{1,0:T(4,128)S(1)}, ...), condition=%wide.region_6.7_spmd.clone, body=%wide.region_0.6_spmd.clone.sunk | while | flops 347014272 | bytes 13164303 | solution.py:103
  110.0 0.6 dynamic_slice.33
  111.3 4.4 %conditional.3 = (f32[4,320]{1,0:T(4,128)S(1)}, f32[4,320]{1,0:T(4,128)S(1)}, f32[4,320,128]{2,1,0:T(8,128)S(1)}) conditional(s32[]{:T(128)} %convert_element_type.74, (s32[4,5,16]{2,1,0:T(8,128)S(1)}, s32[]{:T(128)}, s32[4,5,16]{2,1,0:T(8,128)S(1)}, s32[]{:T(128)}, bf16[5,512,1,128]{3,1,2,0:T(8,128)(2,1)S(1)}, /*index=5*/s32[]{:T(128)}, ...), branch_computations={%region_1.4_spmd, %region_5.5_spmd} | conditional | flops 347014272 | bytes 13151224 | solution.py:99
  111.3 0.6 add_select_fusion
  112.0 0.1 broadcast_compare_fusion.1
  112.0 0.3 and_reduce_fusion
  112.3 0.2 broadcast_in_dim.4
  112.5 0.2 broadcast_compare_fusion
  112.7 0.8 fusion.4
  113.5 1.1 fusion.6
  114.6 1.0 fusion.11
  115.7 0.6 dynamic_slice.33
  117.0 0.6 dynamic_slice.33
  118.4 0.6 dynamic_slice.33
  119.7 0.6 dynamic_slice.33
  121.1 5.3 %fusion.28 = bf16[4096,320]{0,1:T(8,128)(2,1)} fusion(bf16[512,4096]{1,0:T(8,128)(2,1)} %param.15, f32[4,320,128]{2,1,0:T(8,128)S(1)} %get-tuple-element.165, f32[4,320]{1,0:T(4,128)S(1)} %get-tuple-element.166), kind=kOutput, calls=%fused_computation.38 | convolution fusion | flops 1343815680 | bytes 7476224 | tf_op jit(solution)/shard_map/dot_general | solution.py:108
  126.4 0.0 reduce-scatter.2.cloned.1.call-update
  126.4 52.1 %reduce-scatter.2.cloned.1.call-done = bf16[1024,320]{0,1:T(8,128)(2,1)} async-done(((bf16[4096,320]{0,1:T(8,128)(2,1)}), bf16[1024,320]{0,1:T(8,128)(2,1)}) %reduce-scatter.2.cloned.1.call-update) | async-done | bytes 655376 | tf_op jit(solution)/shard_map/reduce_scatter | solution.py:107
  (32 shorter events, 0.3 us)
Async XLA Ops:
  6.5 35.8 %copy-start = (bf16[4096,128]{1,0:T(8,128)(2,1)S(1)}, bf16[4096,128]{1,0:T(8,128)(2,1)}, u32[]{:S(2)}) copy-start(bf16[4096,128]{1,0:T(8,128)(2,1)} %param.13) | copy-start | bytes 3145732
  6.5 30.6 %all-gather.3.cloned.1.call-start = ((), (), s32[]{:S(2)}) async-start(), calls=%async_computation.1 | async-start | bytes 3276800 | tf_op jit(solution)/shard_map/all_gather | solution.py:31
  7.3 171.3 %reduce-scatter.2.cloned.1.call-start = ((), (), s32[]{:S(2)}) async-start(), calls=%async_computation.2 | async-start | bytes 3276800 | tf_op jit(solution)/shard_map/reduce_scatter | solution.py:107
  41.9 1.7 copy-start.1
  43.7 33.6 %copy-start.2 = (bf16[4096,128]{1,0:T(8,128)(2,1)S(1)}, bf16[4096,128]{1,0:T(8,128)(2,1)}, u32[]{:S(2)}) copy-start(bf16[4096,128]{1,0:T(8,128)(2,1)} %param.14) | copy-start | bytes 3145732
  78.1 31.9 %copy-start.3 = (s32[4,5]{1,0:T(4,128)S(1)}, s32[4,5]{1,0:T(4,128)}, u32[]{:S(2)}) copy-start(s32[4,5]{1,0:T(4,128)} %param.17) | copy-start | bytes 244
Sparse Core Ops, SparseCore 0:
  8.9 28.2 all-gather.2
  126.5 51.9 reduce-scatter.1
where the time goes:
time: 186 us; the launch traced here: 185 us
  waiting for transfers between devices  81.4 us (44%)
  blocking collectives  63.3 us (34%)
  between operations  13.5 us (7%)
  matrix products  13.4 us (7%)
  local copies, waits for them, and re-layouts  6.13 us (3%)
  other arithmetic  4.08 us (2%)
  loops' own time  3.5 us (2%)
    reduce_scatter x1, waiting for transfers between devices, on_device(): lax.psum_scatter(lax.dot_general(w_out, flat, (((0,), (1,)), ((), ())), p...  52.1 us
    all_gather x1, blocking collectives, on_device(): key_part = lax.all_gather(keys, 'tok', axis=0, tiled=True)  31.9 us
    all_gather x1, blocking collectives, on_device(): value_part = lax.all_gather(values, 'tok', axis=0, tiled=True)  31.4 us
    all_gather x1, waiting for transfers between devices, on_device(): piece = lax.all_gather(tokens, 'col', axis=1, tiled=True)  28.5 us
    dot_general x3, matrix products, product(): return jnp.dot(piece, weight, preferred_element_type=jnp.float32)  6.19 us
    dot_general x1, matrix products, on_device(): lax.dot_general(w_out, flat, (((0,), (1,)), ((), ())), preferred_element_...  5.31 us
  transfers between devices with their start and end apart: 2, of which 2 were waited for; matrix products, arithmetic and copies ran while one was open for 1% of the time, Pallas kernels for 0%

commit v1 on v0

--- a/solution.py
+++ b/solution.py
@@ -53,8 +53,11 @@
         jnp.zeros((head_local, tok_rows), jnp.float32),
         jnp.zeros((head_local, tok_rows, HEAD_SIZE), jnp.float32),
     )
-    key_part = lax.all_gather(keys, "tok", axis=0, tiled=True)
-    value_part = lax.all_gather(values, "tok", axis=0, tiled=True)
+    key_part, value_part = jnp.split(
+        lax.all_gather(jnp.concatenate([keys, values], axis=1), "tok", axis=0, tiled=True),
+        [keys.shape[1]],
+        axis=1,
+    )
     amount = key_part.shape[0]
     width = 512
     key_blocks = key_part.reshape(amount // width, width, kv_local, HEAD_SIZE)

time: 186 us -> 160 us (0.86)
  blocking collectives: 63.3 us -> 0 us
  waiting for transfers between devices: 81.4 us -> 117 us
  matrix products: 13.4 us -> 15.3 us
    all_gather x2 -> x0, blocking collectives: 63.3 us -> none  [the longest x1 31.9 us: on_device(): key_part = lax.all_gather(keys, 'tok', axis=0, tiled=True)]
    all_gather x0 -> x1, waiting for transfers between devices: none -> 35.7 us  [on_device(): lax.all_gather(jnp.concatenate([keys, values], axis=1), 'tok', axis=0, ti...]
    unnamed x9 -> x11, local copies, waits for them, and re-layouts: 2.04 us -> 0.03 us
    dot_general x3, matrix products: 6.19 us -> 8.07 us  [product(): return jnp.dot(piece, weight, preferred_element_type=jnp.float32)]
  transfers between devices with their start and end apart: 2 -> 3, of which waited for: 2 -> 3; matrix products, arithmetic and copies ran while one was open for 1% -> 4% of each run, Pallas kernels for 0% -> 0%
where the time goes in v1:
time: 160 us; the launch traced here: 159 us
  waiting for transfers between devices  117 us (73%)
  matrix products  15.3 us (10%)
  between operations  13.3 us (8%)
  local copies, waits for them, and re-layouts  5.24 us (3%)
  other arithmetic  4.77 us (3%)
  loops' own time  3.61 us (2%)
    reduce_scatter x1, waiting for transfers between devices, on_device(): lax.psum_scatter(lax.dot_general(w_out, flat, (((0,), (1,)), ((), ())), p...  50.8 us
    all_gather x1, waiting for transfers between devices, on_device(): lax.all_gather(jnp.concatenate([keys, values], axis=1), 'tok', axis=0, ti...  35.7 us
    all_gather x1, waiting for transfers between devices, on_device(): piece = lax.all_gather(tokens, 'col', axis=1, tiled=True)  29.8 us
    dot_general x3, matrix products, product(): return jnp.dot(piece, weight, preferred_element_type=jnp.float32)  8.07 us
    dot_general x1, matrix products, on_device(): lax.dot_general(w_out, flat, (((0,), (1,)), ((), ())), preferred_element_...  5.3 us
    another operation x1, loops' own time, on_device(): lax.scan(one_block, start_state, (key_blocks, value_blocks, offsets))  3.44 us
  transfers between devices with their start and end apart: 3, of which 3 were waited for; matrix products, arithmetic and copies ran while one was open for 4% of the time, Pallas kernels for 0%

profile of v1, /device:TPU:0, one launch (start us, length us, event | category | flops | bytes accessed | tf_op | source)
XLA Modules:
  0.0 159.4 jit_solution(2396049134717326316)
XLA Ops:
  6.5 0.0 copy-start
  6.5 0.0 copy-start.2
  6.5 0.0 all-gather.3.cloned.1.call-start
  6.5 0.7 all-gather.3.cloned.1.call-update
  7.3 0.0 all-gather.5.cloned.1.call-start
  7.3 29.8 %all-gather.3.cloned.1.call-done = bf16[320,4096]{1,0:T(8,128)(2,1)} async-done(((bf16[320,1024]{1,0:T(8,128)(2,1)}), bf16[320,4096]{1,0:T(8,128)(2,1)}) %all-gather.3.cloned.1.call-update) | async-done | bytes 2621456 | tf_op jit(solution)/shard_map/all_gather | solution.py:31
  37.2 0.0 copy-done
  37.2 0.0 copy-start.1
  37.2 2.7 %convolution_bitcast_fusion = f32[320,1,128]{2,0,1:T(8,128)S(1)} fusion(bf16[320,4096]{1,0:T(8,128)(2,1)} %all-gather.3.cloned.1.call-done, bf16[4096,128]{1,0:T(8,128)(2,1)S(1)} %copy-done), kind=kOutput, calls=%fused_computation.39 | convolution fusion | flops 335544320 | bytes 3833856 | tf_op jit(solution)/shard_map/dot_general | solution.py:35
  39.9 0.0 copy-start.4
  39.9 0.7 fusion.40
  40.7 0.0 copy-done.2
  40.7 0.0 copy-done.1
  40.7 0.8 fusion.29
  41.5 0.8 pad_maximum_fusion.1
  42.3 0.0 all-gather.5.cloned.1.call-update
  42.3 0.0 reduce-scatter.2.cloned.1.call-start
  42.4 0.0 copy-done.4
  42.4 0.6 multiply_cosine_fusion
  43.0 4.5 %fusion.45 = f32[320,512]{1,0:T(8,128)S(1)} fusion(bf16[320,4096]{1,0:T(8,128)(2,1)} %all-gather.3.cloned.1.call-done, bf16[4096,512]{1,0:T(8,128)(2,1)} %param.12), kind=kOutput, calls=%fused_computation.69 | convolution fusion | flops 1342177280 | bytes 7471104 | tf_op jit(solution)/shard_map/dot_general | solution.py:35
  47.5 0.2 reshape.339
  47.8 0.4 fusion.44
  48.2 0.2 fusion.30
  48.4 0.0 copy-start.3
  48.4 0.2 pad_maximum_fusion
  48.6 35.7 %all-gather.5.cloned.1.call-done = bf16[2560,2,128]{2,0,1:T(8,128)(2,1)} async-done(((bf16[320,2,128]{2,0,1:T(8,128)(2,1)}), bf16[2560,2,128]{2,0,1:T(8,128)(2,1)}) %all-gather.5.cloned.1.call-update) | async-done | bytes 1310736 | tf_op jit(solution)/shard_map/all_gather | solution.py:57
  84.3 1.4 fusion.43
  85.7 0.0 copy-done.3
  85.7 10.9 %while.15 = (s32[]{:T(128)}, f32[4,320]{1,0:T(4,128)S(1)}, f32[4,320]{1,0:T(4,128)S(1)}, f32[4,320,128]{2,1,0:T(8,128)S(1)}, s32[5]{0:T(128)S(1)}, /*index=5*/s3...) while((s32[]{:T(128)}, f32[4,320]{1,0:T(4,128)S(1)}, ...), condition=%wide.region_6.7_spmd.clone, body=%wide.region_0.6_spmd.clone.sunk | while | flops 347014272 | bytes 13164303 | solution.py:106
  85.7 0.6 dynamic_slice.33
  87.0 4.4 %conditional.3 = (f32[4,320]{1,0:T(4,128)S(1)}, f32[4,320]{1,0:T(4,128)S(1)}, f32[4,320,128]{2,1,0:T(8,128)S(1)}) conditional(s32[]{:T(128)} %convert_element_type.76, (s32[4,5,16]{2,1,0:T(8,128)S(1)}, s32[]{:T(128)}, s32[4,5,16]{2,1,0:T(8,128)S(1)}, s32[]{:T(128)}, bf16[5,512,1,128]{3,1,2,0:T(8,128)(2,1)S(1)}, /*index=5*/s32[]{:T(128)}, ...), branch_computations={%region_1.4_spmd, %region_5.5_spmd} | conditional | flops 347014272 | bytes 13151224 | solution.py:102
  87.0 0.7 add_select_fusion
  87.7 0.1 broadcast_compare_fusion.1
  87.7 0.3 and_reduce_fusion
  88.0 0.2 broadcast_in_dim.4
  88.2 0.2 broadcast_compare_fusion
  88.4 0.8 fusion.4
  89.2 1.1 fusion.6
  90.3 1.0 fusion.11
  91.4 0.6 dynamic_slice.33
  92.7 0.6 dynamic_slice.33
  94.0 0.6 dynamic_slice.33
  95.4 0.6 dynamic_slice.33
  96.7 5.3 %fusion.28 = bf16[4096,320]{0,1:T(8,128)(2,1)} fusion(bf16[512,4096]{1,0:T(8,128)(2,1)} %param.15, f32[4,320,128]{2,1,0:T(8,128)S(1)} %get-tuple-element.165, f32[4,320]{1,0:T(4,128)S(1)} %get-tuple-element.166), kind=kOutput, calls=%fused_computation.38 | convolution fusion | flops 1343815680 | bytes 7476224 | tf_op jit(solution)/shard_map/dot_general | solution.py:111
  102.0 0.0 reduce-scatter.2.cloned.1.call-update
  102.0 50.8 %reduce-scatter.2.cloned.1.call-done = bf16[1024,320]{0,1:T(8,128)(2,1)} async-done(((bf16[4096,320]{0,1:T(8,128)(2,1)}), bf16[1024,320]{0,1:T(8,128)(2,1)}) %reduce-scatter.2.cloned.1.call-update) | async-done | bytes 655376 | tf_op jit(solution)/shard_map/reduce_scatter | solution.py:110
  (33 shorter events, 0.3 us)
Async XLA Ops:
  6.5 30.7 %copy-start = (bf16[4096,128]{1,0:T(8,128)(2,1)S(1)}, bf16[4096,128]{1,0:T(8,128)(2,1)}, u32[]{:S(2)}) copy-start(bf16[4096,128]{1,0:T(8,128)(2,1)} %param.13) | copy-start | bytes 3145732
  6.5 34.1 %copy-start.2 = (bf16[4096,128]{1,0:T(8,128)(2,1)S(1)}, bf16[4096,128]{1,0:T(8,128)(2,1)}, u32[]{:S(2)}) copy-start(bf16[4096,128]{1,0:T(8,128)(2,1)} %param.14) | copy-start | bytes 3145732
  6.5 30.6 %all-gather.3.cloned.1.call-start = ((), (), s32[]{:S(2)}) async-start(), calls=%async_computation.1 | async-start | bytes 3276800 | tf_op jit(solution)/shard_map/all_gather | solution.py:31
  7.3 77.0 %all-gather.5.cloned.1.call-start = ((), (), s32[]{:S(2)}) async-start(), calls=%async_computation.2 | async-start | bytes 1474560 | tf_op jit(solution)/shard_map/all_gather | solution.py:57
  37.2 3.5 %copy-start.1 = (bf16[320,4096]{1,0:T(8,128)(2,1)S(1)}, bf16[320,4096]{1,0:T(8,128)(2,1)}, u32[]{:S(2)}) copy-start(bf16[320,4096]{1,0:T(8,128)(2,1)} %all-gather.3.cloned.1.call-done) | copy-start | bytes 7864324
  39.9 2.4 %copy-start.4 = (s32[4,5,16]{2,0,1:T(4,128)S(1)}, s32[4,5,16]{2,0,1:T(4,128)}, u32[]{:S(2)}) copy-start(s32[4,5,16]{2,0,1:T(4,128)} %param.16) | copy-start | bytes 3844
  42.3 110.5 %reduce-scatter.2.cloned.1.call-start = ((), (), s32[]{:S(2)}) async-start(), calls=%async_computation.3 | async-start | bytes 3276800 | tf_op jit(solution)/shard_map/reduce_scatter | solution.py:110
  48.4 37.4 %copy-start.3 = (s32[4,5]{1,0:T(4,128)S(1)}, s32[4,5]{1,0:T(4,128)}, u32[]{:S(2)}) copy-start(s32[4,5]{1,0:T(4,128)} %param.17) | copy-start | bytes 244
Sparse Core Ops, SparseCore 0:
  8.9 28.2 all-gather.2
  42.4 41.7 all-gather.4
  102.1 50.6 reduce-scatter.1
